TPU v7x, 32 devices: a whole 2x2x4 slice. The times are simulated.
32 devices in a mesh: run: 8 (over z, y), rep: 4 (over x, core).
Axes of the slice: x: 2, y: 2, z: 4, core: 2. Of those that a mesh axis runs over, the one named last changes fastest.
Arguments:
- edge_feats: bfloat16 [4, 16384, 1280], P('rep', 'run'), may hold values from -6 to 6
- edge_grads: bfloat16 [4, 16384, 640], P('rep', 'run'), may hold values from -0.059814453 to 0.059814453
- edge_system: int32 [4, 16384], P('rep', 'run'), may hold values from 0 to 5, as said below
- edge_count: int32 [4, 8], P('rep', 'run'), may hold values from 1025 to 2048
- coef: float32 [4, 6, 32], P('rep'), may hold values from 0.05 to 1
- weights: float32 [32, 1280, 640], P('rep', 'run'), may hold values from -0.15625 to 0.15625
- first_moment: float32 [32, 1280, 640], P('rep', 'run'), may hold values from -6 to 6
- second_moment: float32 [32, 1280, 640], P('rep', 'run'), may hold values from 1 to 10
Outputs:
- new_weights: float32 [32, 1280, 640], P('rep', 'run')
- new_first: float32 [32, 1280, 640], P('rep', 'run')
- new_second: float32 [32, 1280, 640], P('rep', 'run')
- merged_next: bfloat16 [4, 6, 1280, 640], P('rep', None, 'run')
Inputs may be any that keep to these rules, and one draw needn't show every extreme that they name: `edge_system`: along each replica's rows the system never falls; every system number appears; the live rows of one device belong to one or two systems, two on some device in every draw.
All inputs are finite; a program needn't handle non-finite values.
Results may differ from a plain program's by a relative error of at most 0.001.
The roundings to bfloat16 on the way count: a program that leaves them out, or rounds other values in their place, can miss the bound.
Values may be sent and summed in bfloat16 or wider, within the bound.
A program may use at most 128 MiB of HBM per device.

v0:
```python
import jax
import jax.numpy as jnp
from jax import lax
from jax.sharding import PartitionSpec as P


def on_device(
    edge_feats, edge_grads, edge_system, edge_count, coef, weights, first_moment, second_moment
):
    feats = edge_feats[0]
    grads = edge_grads[0]
    system = edge_system[0]
    live_count = edge_count[0, 0]
    group_coef = coef[0]
    nsys = group_coef.shape[0]
    rows = system.shape[0]
    live = jnp.arange(rows) < live_count
    first = system[0]
    last = lax.dynamic_index_in_dim(system, live_count - 1, 0, keepdims=False)
    has_upper = last > first
    empty = jnp.zeros_like(grads)

    def slot_grad(offset):
        keep = live & (system == first + offset)
        right = jnp.where(keep[:, None], grads, empty)
        return lax.dot_general(
            feats, right, (((0,), (0,)), ((), ())), preferred_element_type=jnp.float32
        )

    lower = slot_grad(0)
    upper = lax.cond(has_upper, lambda: slot_grad(1), lambda: jnp.zeros_like(lower))
    stacked = jnp.stack([lower, upper])
    pieces = lax.all_to_all(stacked, "run", split_axis=1, concat_axis=0, tiled=True)
    high_index = jnp.minimum(first + 1, nsys - 1)
    slot_coef = jnp.stack(
        [group_coef[first], group_coef[high_index] * has_upper.astype(jnp.float32)]
    )
    all_coef = lax.all_gather(slot_coef, "run", axis=0, tiled=True)
    mixed = jnp.einsum("ke,kio->eio", all_coef, pieces, precision=lax.Precision.HIGHEST)
    expert_grad = lax.psum_scatter(mixed, "rep", scatter_dimension=0, tiled=True)
    new_first = 0.9 * first_moment + 0.1 * expert_grad
    new_second = 0.999 * second_moment + 0.001 * expert_grad * expert_grad
    corr_first = 1.0 - 0.9**10
    corr_second = 1.0 - 0.999**10
    new_weights = weights - 0.01 * (new_first / corr_first) / (
        jnp.sqrt(new_second / corr_second) + 1e-08
    )
    rounded = lax.optimization_barrier(new_weights.astype(jnp.bfloat16))
    every_expert = lax.all_gather(rounded, "rep", axis=0, tiled=True)
    experts, din_local, dout = every_expert.shape
    flat = every_expert.astype(jnp.float32).reshape(experts, din_local * dout)
    merged = jnp.dot(group_coef, flat, precision=lax.Precision.HIGHEST)
    merged_next = merged.reshape(nsys, din_local, dout).astype(jnp.bfloat16)
    return (new_weights, new_first, new_second, merged_next[None])


def solution(mesh):
    placed = (
        P("rep", "run", None),
        P("rep", "run", None),
        P("rep", "run"),
        P("rep", "run"),
        P("rep", None, None),
        P("rep", "run", None),
        P("rep", "run", None),
        P("rep", "run", None),
    )
    return jax.shard_map(
        on_device,
        mesh=mesh,
        in_specs=placed,
        out_specs=(
            P("rep", "run", None),
            P("rep", "run", None),
            P("rep", "run", None),
            P("rep", None, "run", None),
        ),
        check_vma=False,
    )
```

profile of v0, /device:TPU:13, one launch (start us, length us, event | category | flops | bytes accessed | tf_op | source)
XLA Modules:
  0.0 417.6 jit_solution(7868111956152384483)
XLA Ops:
  7.8 1.3 constant_dynamic-slice_fusion
  9.1 1.4 compare_reduce_fusion.1
  11.8 8.7 %convolution_bitcast_fusion.1 = f32[1,1280,640]{1,2,0:T(8,128)} fusion(bf16[1,2048,640]{2,1,0:T(8,128)(2,1)} %param.11, pred[2048]{0:T(1024)(128)(4,1)S(1)} %fusion.9, bf16[1,2048,1280]{2,1,0:T(8,128)(2,1)} %param.10), kind=kOutput, calls=%fused_computation.10 | convolution fusion | flops 3356753920 | bytes 11143168 | tf_op jit(solution)/shard_map/dot_general | solution.py:26
  20.5 8.4 %conditional.1 = (f32[1,1280,640]{1,2,0:T(8,128)S(1)}) conditional(s32[]{:T(128)} %convert_element_type.27, () %tuple.16, (s32[]{:T(128)}, s32[2048]{0:T(1024)S(1)}, s32[]{:T(128)}, s32[1,2048]{1,0:T(1,128)S(1)}, bf16[1,2048,640]{2,1,0:T(8,128)(2,1)}, /*index=5*/bf16[2048,1280]{1,0:T(8,128)(2,1)}) %tuple.34), branch_computations={%region_0.1_spmd, %region_1.2_spmd} | conditional | flops 3356760064 | bytes 11165724 | solution.py:31
  21.2 0.7 compare_and_fusion
  21.9 7.0 %convolution_bitcast_fusion = f32[1,1280,640]{1,2,0:T(8,128)S(1)} fusion(bf16[2048,1280]{1,0:T(8,128)(2,1)} %get-tuple-element.25, bf16[1,2048,640]{2,1,0:T(8,128)(2,1)} %get-tuple-element.24, pred[2048]{0:T(1024)(128)(4,1)S(1)} %compare_and_fusion), kind=kOutput, calls=%fused_computation | convolution fusion | flops 3356753920 | bytes 11143168 | tf_op jit(solution)/shard_map/cond/branch_1_fun/dot_general | solution.py:26
  28.9 5.1 %pad_maximum_fusion = f32[2,1280,640]{1,2,0:T(8,128)} fusion(f32[1,1280,640]{1,2,0:T(8,128)S(1)} %get-tuple-element.50, f32[1,1280,640]{1,2,0:T(8,128)} %convolution_bitcast_fusion.1), kind=kLoop, calls=%fused_computation.8 | loop fusion | flops 1638400 | bytes 13107200 | tf_op jit(solution)/shard_map/stack | solution.py:32
  34.0 11.9 %copy.29 = f32[2,1280,640]{2,0,1:T(2,128)} copy(f32[2,1280,640]{1,2,0:T(8,128)} %pad_maximum_fusion) | data formatting | bytes 13107200 | tf_op jit(solution)/shard_map/stack | solution.py:32
  46.0 5.8 %all-to-all-start = ((f32[2,1280,640]{2,0,1:T(2,128)}), f32[2,1280,640]{2,0,1:T(2,128)}, u32[]{:S(2)}, u32[]{:S(2)}) async-start(f32[2,1280,640]{2,0,1:T(2,128)} %copy.29), calls=%async_computation | async-start | bytes 13107200 | tf_op jit(solution)/shard_map/all_to_all | solution.py:33
  54.4 145.6 %all-gather = f32[8,2,32]{2,1,0:T(2,128)S(1)} all-gather(f32[1,2,32]{2,1,0:T(2,128)S(1)} %maximum_bitcast_fusion), channel_id=1, replica_groups=mesh['run'=8,'rep'=4] {'run'}, dimensions={0}, use_global_device_ids=true | all-gather | bytes 2304 | tf_op jit(solution)/shard_map/all_gather | solution.py:38
  200.0 6.0 %copy.30 = f32[2,1280,640]{2,1,0:T(8,128)} copy(f32[2,1280,640]{2,0,1:T(2,128)} %all-to-all-done) | data formatting | bytes 13107200 | tf_op jit(solution)/shard_map/all_to_all | solution.py:33
  206.0 10.6 %copy.31 = f32[8,2,160,640]{3,1,0,2:T(2,128)} copy(f32[8,2,160,640]{3,2,0,1:T(8,128)} %bitcast.53) | data formatting | bytes 13107200 | tf_op jit(solution)/shard_map/all_to_all | solution.py:33
  216.7 8.6 %all_to_all.16 = f32[16,160,640]{2,0,1:T(8,128)} reshape(f32[8,2,160,640]{3,1,0,2:T(2,128)} %copy.31) | data formatting | bytes 13107200 | tf_op jit(solution)/shard_map/all_to_all | solution.py:33
  225.3 14.2 %fusion.20 = f32[32,160,640]{2,0,1:T(8,128)} fusion(f32[16,32,1]{1,0,2:T(8,128)S(1)} %bitcast.56, f32[16,160,640]{2,0,1:T(8,128)} %all_to_all.16), kind=kOutput, calls=%fused_computation.36 | convolution fusion | flops 629145600 | bytes 19662848 | tf_op jit(solution)/shard_map/ke,kio->eio/dot_general | solution.py:39
  239.6 0.3 all-gather.3.cloned.1.call-start
  239.8 102.8 %reduce-scatter.2.cloned.1.call-done = f32[8,160,640]{2,0,1:T(8,128)} async-done(((f32[32,160,640]{2,0,1:T(8,128)}), f32[8,160,640]{2,0,1:T(8,128)}) %reduce-scatter.2.cloned.1.call-update) | async-done | bytes 3276816 | tf_op jit(solution)/shard_map/reduce_scatter | solution.py:40
  342.6 12.3 %fusion.17 = (bf16[8,160,640]{2,0,1:T(8,128)(2,1)}, f32[8,160,640]{2,0,1:T(8,128)}, f32[8,160,640]{2,0,1:T(8,128)}, f32[8,160,640]{2,0,1:T(8,128)S(1)}) fusion(f32[8,160,640]{2,1,0:T(8,128)} %param.15, f32[8,160,640]{2,0,1:T(8,128)} %reduce-scatter.2.cloned.1.call-done, f32[8,160,640]{2,1,0:T(8,128)} %param.16, f32[8,160,640]{2,1,0:T(8,128)} %param.17), kind=kLoop, calls=%fused_computation.35 | loop fusion | flops 10649600 | bytes 24576000 | tf_op jit(solution)/shard_map/convert_element_type | solution.py:48
  355.0 4.4 %copy.35 = f32[8,160,640]{2,1,0:T(8,128)} copy(f32[8,160,640]{2,0,1:T(8,128)} %get-tuple-element.43) | data formatting | bytes 6553600
  359.4 2.3 copy.36
  361.7 2.3 copy.37
  364.0 39.5 %all-gather.3.cloned.1.call-done = bf16[32,160,640]{2,0,1:T(8,128)(2,1)} async-done(((bf16[8,160,640]{2,0,1:T(8,128)(2,1)}), bf16[32,160,640]{2,0,1:T(8,128)(2,1)}) %all-gather.3.cloned.1.call-update) | async-done | bytes 6553616 | tf_op jit(solution)/shard_map/all_gather | solution.py:49
  403.5 3.4 copy.39
  406.9 2.7 convolution_convert_fusion
  409.6 1.2 copy.56
  (15 shorter events, 0.1 us)
Async XLA Ops:
  11.8 8.8 %copy-start.1 = (s32[1,2048]{1,0:T(1,128)S(1)}, s32[1,2048]{1,0:T(1,128)}, u32[]{:S(2)}) copy-start(s32[1,2048]{1,0:T(1,128)} %param.12) | copy-start | bytes 24580
  46.0 8.4 %copy-start.2 = (f32[1,6,32]{2,0,1:T(1,128)S(1)}, f32[1,6,32]{2,0,1:T(1,128)}, u32[]{:S(2)}) copy-start(f32[1,6,32]{2,0,1:T(1,128)} %param.14) | copy-start | bytes 2308
  46.0 154.1 %all-to-all-start = ((f32[2,1280,640]{2,0,1:T(2,128)}), f32[2,1280,640]{2,0,1:T(2,128)}, u32[]{:S(2)}, u32[]{:S(2)}) async-start(f32[2,1280,640]{2,0,1:T(2,128)} %copy.29), calls=%async_computation | async-start | bytes 13107200 | tf_op jit(solution)/shard_map/all_to_all | solution.py:33
  51.8 290.9 %reduce-scatter.2.cloned.1.call-start = ((), (), s32[]{:S(2)}) async-start(), calls=%async_computation.2 | async-start | bytes 16384000 | tf_op jit(solution)/shard_map/reduce_scatter | solution.py:40
  239.6 164.0 %all-gather.3.cloned.1.call-start = ((), (), s32[]{:S(2)}) async-start(), calls=%async_computation.3 | async-start | bytes 8192000 | tf_op jit(solution)/shard_map/all_gather | solution.py:49
  355.0 4.4 %copy-start = (f32[8,160,640]{2,0,1:T(8,128)S(1)}, f32[8,160,640]{2,0,1:T(8,128)}, u32[]{:S(2)}) copy-start(f32[8,160,640]{2,0,1:T(8,128)} %get-tuple-element.44) | copy-start | bytes 9830404
Sparse Core Ops, SparseCore 0:
  239.7 102.9 reduce-scatter.1
  355.1 48.3 all-gather.2
where the time goes:
time: 420 us; the launch traced here: 418 us
  blocking collectives  146 us (35%)
  waiting for transfers between devices  142 us (34%)
  local copies, waits for them, and re-layouts  52.1 us (12%)
  matrix products  32.7 us (8%)
  other arithmetic  19.5 us (5%)
  between operations  18.6 us (4%)
  starting transfers between devices  6.06 us (1%)
    all_gather x1, blocking collectives, on_device(): all_coef = lax.all_gather(slot_coef, 'run', axis=0, tiled=True)  146 us
    reduce_scatter x1, waiting for transfers between devices, on_device(): lax.psum_scatter(mixed, 'rep', scatter_dimension=0, tiled=True)  103 us
    all_gather x1, waiting for transfers between devices, on_device(): every_expert = lax.all_gather(rounded, 'rep', axis=0, tiled=True)  39.5 us
    all_to_all x3, local copies, waits for them, and re-layouts, on_device(): lax.all_to_all(stacked, 'run', split_axis=1, concat_axis=0, tiled=True)  25.3 us
    dot_general x2, matrix products, slot_grad(): lax.dot_general(feats, right, (((0,), (0,)), ((), ())), preferred_element...  15.8 us
    dot_general x1, matrix products, on_device(): jnp.einsum('ke,kio->eio', all_coef, pieces, precision=lax.Precision.HIGHEST)  14.2 us
    convert_element_type x1, other arithmetic, on_device(): rounded = lax.optimization_barrier(new_weights.astype(jnp.bfloat16))  12.3 us
    another operation x1, local copies, waits for them, and re-layouts, on_device(): stacked = jnp.stack([lower, upper])  11.9 us
  transfers between devices with their start and end apart: 3, of which 2 were waited for; matrix products, arithmetic and copies ran while one was open for 2% of the time, Pallas kernels for 0%

commit v1 on v0

--- a/solution.py
+++ b/solution.py
@@ -16,28 +16,34 @@
     rows = system.shape[0]
     live = jnp.arange(rows) < live_count
     first = system[0]
-    last = lax.dynamic_index_in_dim(system, live_count - 1, 0, keepdims=False)
-    has_upper = last > first
     empty = jnp.zeros_like(grads)
-
-    def slot_grad(offset):
-        keep = live & (system == first + offset)
-        right = jnp.where(keep[:, None], grads, empty)
-        return lax.dot_general(
-            feats, right, (((0,), (0,)), ((), ())), preferred_element_type=jnp.float32
-        )
-
-    lower = slot_grad(0)
-    upper = lax.cond(has_upper, lambda: slot_grad(1), lambda: jnp.zeros_like(lower))
-    stacked = jnp.stack([lower, upper])
-    pieces = lax.all_to_all(stacked, "run", split_axis=1, concat_axis=0, tiled=True)
-    high_index = jnp.minimum(first + 1, nsys - 1)
-    slot_coef = jnp.stack(
-        [group_coef[first], group_coef[high_index] * has_upper.astype(jnp.float32)]
+    lower = jnp.where((live & (system == first))[:, None], grads, empty)
+    upper = jnp.where((live & (system == first + 1))[:, None], grads, empty)
+    right = jnp.concatenate([lower, upper], axis=1)
+    slots = lax.dot_general(
+        feats, right, (((0,), (0,)), ((), ())), preferred_element_type=jnp.float32
+    ).astype(jnp.bfloat16)
+    pieces = lax.all_to_all(slots, "run", split_axis=0, concat_axis=0, tiled=True)
+    firsts = lax.all_gather(first, "run")
+    n_run = firsts.shape[0]
+    pieces = pieces.reshape(n_run, -1, pieces.shape[1])
+    dout = grads.shape[1]
+    sums = []
+    for s in range(nsys):
+        total = 0.0
+        for k in range(n_run):
+            low = pieces[k, :, :dout].astype(jnp.float32)
+            high = pieces[k, :, dout:].astype(jnp.float32)
+            total = total + jnp.where(firsts[k] == s, low, 0.0)
+            total = total + jnp.where(firsts[k] + 1 == s, high, 0.0)
+        sums.append(total.astype(jnp.bfloat16))
+    every_sum = lax.all_gather(jnp.stack(sums), "rep", axis=0, tiled=True)
+    every_coef = lax.all_gather(group_coef, "rep", axis=0, tiled=True)
+    held = weights.shape[0]
+    own_coef = lax.dynamic_slice_in_dim(every_coef, lax.axis_index("rep") * held, held, 1)
+    expert_grad = jnp.einsum(
+        "ge,gio->eio", own_coef, every_sum.astype(jnp.float32), precision=lax.Precision.HIGHEST
     )
-    all_coef = lax.all_gather(slot_coef, "run", axis=0, tiled=True)
-    mixed = jnp.einsum("ke,kio->eio", all_coef, pieces, precision=lax.Precision.HIGHEST)
-    expert_grad = lax.psum_scatter(mixed, "rep", scatter_dimension=0, tiled=True)
     new_first = 0.9 * first_moment + 0.1 * expert_grad
     new_second = 0.999 * second_moment + 0.001 * expert_grad * expert_grad
     corr_first = 1.0 - 0.9**10

time: 420 us -> 266 us (0.63)
  blocking collectives: 146 us -> 74.9 us
  waiting for transfers between devices: 142 us -> 73.9 us
  local copies, waits for them, and re-layouts: 52.1 us -> 17.5 us
  between operations: 18.6 us -> 50.7 us
  other arithmetic: 19.5 us -> 13 us
  matrix products: 32.7 us -> 28 us
    all_gather x1, blocking collectives: 146 us -> 5.74 us  [on_device(): every_coef = lax.all_gather(group_coef, 'rep', axis=0, tiled=True)]
    reduce_scatter x1 -> x0, waiting for transfers between devices: 103 us -> none  [on_device(): lax.psum_scatter(mixed, 'rep', scatter_dimension=0, tiled=True)]
    unnamed x0 -> x1, blocking collectives: none -> 69.2 us
    all_gather x0 -> x1, waiting for transfers between devices: none -> 34.9 us  [on_device(): every_sum = lax.all_gather(jnp.stack(sums), 'rep', axis=0, tiled=True)]
    all_to_all x3 -> x0, local copies, waits for them, and re-layouts: 25.3 us -> none  [on_device(): lax.all_to_all(stacked, 'run', split_axis=1, concat_axis=0, tiled=True)]
    convert_element_type x1 -> x0, other arithmetic: 12.3 us -> none  [on_device(): rounded = lax.optimization_barrier(new_weights.astype(jnp.bfloat16))]
    another operation x1 -> x0, local copies, waits for them, and re-layouts: 11.9 us -> none  [on_device(): stacked = jnp.stack([lower, upper])]
    unnamed x1 -> x5, other arithmetic: 0.01 us -> 6.61 us
  transfers between devices with their start and end apart: 3 -> 3, of which waited for: 2 -> 2; matrix products, arithmetic and copies ran while one was open for 2% -> 4% of each run, Pallas kernels for 0% -> 0%
where the time goes in v1:
time: 266 us; the launch traced here: 264 us
  blocking collectives  74.9 us (28%)
  waiting for transfers between devices  73.9 us (28%)
  between operations  50.7 us (19%)
  matrix products  28 us (11%)
  local copies, waits for them, and re-layouts  17.5 us (7%)
  other arithmetic  13 us (5%)
  starting transfers between devices  5.84 us (2%)
    unnamed x1, blocking collectives  69.2 us
    all_gather x1, waiting for transfers between devices, on_device(): every_expert = lax.all_gather(rounded, 'rep', axis=0, tiled=True)  38.9 us
    all_gather x1, waiting for transfers between devices, on_device(): every_sum = lax.all_gather(jnp.stack(sums), 'rep', axis=0, tiled=True)  34.9 us
    dot_general x1, matrix products, on_device(): jnp.einsum('ge,gio->eio', own_coef, every_sum.astype(jnp.float32), precis...  16.8 us
    unnamed x15, local copies, waits for them, and re-layouts  12.1 us
    dot_general x1, matrix products, on_device(): lax.dot_general(feats, right, (((0,), (0,)), ((), ())), preferred_element...  8.52 us
    unnamed x5, other arithmetic  6.61 us
    all_to_all x1, starting transfers between devices, on_device(): lax.all_to_all(slots, 'run', split_axis=0, concat_axis=0, tiled=True)  5.79 us
  transfers between devices with their start and end apart: 3, of which 2 were waited for; matrix products, arithmetic and copies ran while one was open for 4% of the time, Pallas kernels for 0%

profile of v1, /device:TPU:13, one launch (start us, length us, event | category | flops | bytes accessed | tf_op | source)
XLA Modules:
  0.0 263.8 jit_solution(6551569824041858557)
XLA Ops:
  7.8 1.2 slice.53
  9.6 1.4 compare_reduce_fusion.1
  11.1 3.7 %bitcast_select_fusion.1 = (bf16[2048,640]{1,0:T(8,128)(2,1)S(1)}, bf16[2048,640]{1,0:T(8,128)(2,1)S(1)}) fusion(bf16[1,2048,640]{2,1,0:T(8,128)(2,1)} %param.9, pred[2048]{0:T(1024)(128)(4,1)S(1)} %get-tuple-element.33, pred[2048]{0:T(1024)(128)(4,1)S(1)} %get-tuple-element.32), kind=kLoop, calls=%fused_computation.15 | loop fusion | flops 2621440 | bytes 7868416 | tf_op jit(solution)/shard_map/jit(_where)/select_n | solution.py:20
  14.8 8.5 %convolution_convert_fusion.1 = bf16[1280,1280]{0,1:T(8,128)(2,1)} fusion(bf16[2048,640]{1,0:T(8,128)(2,1)S(1)} %get-tuple-element.23, bf16[2048,640]{1,0:T(8,128)(2,1)S(1)} %get-tuple-element.22, bf16[1,2048,1280]{2,1,0:T(8,128)(2,1)S(1)} %copy-done.2), kind=kOutput, calls=%fused_computation.1 | convolution fusion | flops 6723010560 | bytes 13762560 | tf_op jit(solution)/shard_map/dot_general | solution.py:23
  23.3 5.8 %all-to-all-start = ((bf16[8,160,1280]{2,1,0:T(8,128)(2,1)}), bf16[8,160,1280]{2,1,0:T(8,128)(2,1)S(1)}, u32[]{:S(2)}, u32[]{:S(2)}) async-start(bf16[8,160,1280]{2,1,0:T(8,128)(2,1)} %bitcast.130), calls=%async_computation | async-start | bytes 6553600 | tf_op jit(solution)/shard_map/all_to_all | solution.py:26
  29.7 1.3 bitcast_dynamic-update-slice_fusion
  31.0 69.2 %all-reduce = s32[8]{0:T(128)S(1)} all-reduce(s32[8]{0:T(128)S(1)} %bitcast_dynamic-update-slice_fusion), channel_id=3, replica_groups=mesh['run'=8,'rep'=4] {'run'}, use_global_device_ids=true, to_apply=%add | all-reduce | flops 8 | bytes 64
  100.2 0.7 fusion.118
  136.1 1.3 fusion.104
  137.4 1.3 fusion.105
  138.7 1.3 fusion.106
  140.1 1.3 fusion.107
  141.4 1.3 fusion.108
  142.7 1.3 fusion.109
  144.1 5.7 %all-gather = f32[1,24,32]{2,0,1:T(1,128)S(1)} all-gather(f32[1,6,32]{2,0,1:T(1,128)S(1)} %copy-done.1), channel_id=2, replica_groups=mesh['run'=8,'rep'=4] {'rep'}, dimensions={1}, use_global_device_ids=true | all-gather | bytes 3840 | tf_op jit(solution)/shard_map/all_gather | solution.py:41
  149.9 34.9 %all-gather.5.cloned.1.call-done = bf16[24,160,640]{2,1,0:T(8,128)(2,1)} async-done(((bf16[6,160,640]{2,1,0:T(8,128)(2,1)}), bf16[24,160,640]{2,1,0:T(8,128)(2,1)}) %all-gather.5.cloned.1.call-update) | async-done | bytes 4915216 | tf_op jit(solution)/shard_map/all_gather | solution.py:40
  184.9 16.8 %fusion.115 = (bf16[8,160,640]{2,0,1:T(8,128)(2,1)}, f32[8,160,640]{2,0,1:T(8,128)}, f32[8,160,640]{2,0,1:T(8,128)}, f32[8,160,640]{2,0,1:T(8,128)S(1)}) fusion(f32[8,160,640]{2,1,0:T(8,128)} %param.13, f32[8,160,640]{2,1,0:T(8,128)} %param.14, f32[8,160,640]{2,1,0:T(8,128)} %param.15, f32[24,8,1]{1,0,2:T(8,128)S(1)} %bitcast.131, ...), kind=kOutput, calls=%fused_computation.225 | convolution fusion | flops 246579200 | bytes 26215168 | tf_op jit(solution)/shard_map/ge,gio->eio/dot_general | solution.py:44
  201.7 4.4 %copy.35 = f32[8,160,640]{2,1,0:T(8,128)} copy(f32[8,160,640]{2,0,1:T(8,128)} %get-tuple-element.19) | data formatting | bytes 6553600
  206.1 2.3 copy.36
  208.4 2.3 copy.37
  210.7 38.9 %all-gather.7.cloned.1.call-done = bf16[32,160,640]{2,0,1:T(8,128)(2,1)} async-done(((bf16[8,160,640]{2,0,1:T(8,128)(2,1)}), bf16[32,160,640]{2,0,1:T(8,128)(2,1)}) %all-gather.7.cloned.1.call-update) | async-done | bytes 6553616 | tf_op jit(solution)/shard_map/all_gather | solution.py:55
  249.7 3.4 %copy.39 = bf16[160,4,8,640]{3,2,0,1:T(8,128)(2,1)S(1)} copy(bf16[160,4,8,640]{3,2,1,0:T(8,128)(2,1)} %bitcast.129) | data formatting | bytes 13107200 | tf_op jit(solution)/shard_map/reshape | solution.py:57
  253.1 2.7 %convolution_convert_fusion = bf16[102400,6]{0,1:T(8,128)(2,1)S(1)} fusion(bf16[32,102400]{1,0:T(8,128)(2,1)S(1)} %bitcast.127, f32[1,6,32]{2,0,1:T(1,128)S(1)} %copy-done.1), kind=kOutput, calls=%fused_computation | convolution fusion | flops 236544000 | bytes 7783168 | tf_op jit(solution)/shard_map/dot_general | solution.py:58
  255.7 1.2 copy.60
  (17 shorter events, 0.8 us)
Async XLA Ops:
  11.0 3.7 %copy-start.2 = (bf16[1,2048,1280]{2,1,0:T(8,128)(2,1)S(1)}, bf16[1,2048,1280]{2,1,0:T(8,128)(2,1)}, u32[]{:S(2)}) copy-start(bf16[1,2048,1280]{2,1,0:T(8,128)(2,1)} %param.8) | copy-start | bytes 15728644
  23.3 5.8 %copy-start.3 = (u32[32]{0:T(128)S(1)}, u32[32]{0:T(128)}, u32[]{:S(2)}) copy-start(u32[32]{0:T(128)} %constant.260) | copy-start | bytes 388
  23.3 112.8 %all-to-all-start = ((bf16[8,160,1280]{2,1,0:T(8,128)(2,1)}), bf16[8,160,1280]{2,1,0:T(8,128)(2,1)S(1)}, u32[]{:S(2)}, u32[]{:S(2)}) async-start(bf16[8,160,1280]{2,1,0:T(8,128)(2,1)} %bitcast.130), calls=%async_computation | async-start | bytes 6553600 | tf_op jit(solution)/shard_map/all_to_all | solution.py:26
  29.1 155.8 %all-gather.5.cloned.1.call-start = ((), (), s32[]{:S(2)}) async-start(), calls=%async_computation.1 | async-start | bytes 6144000 | tf_op jit(solution)/shard_map/all_gather | solution.py:40
  141.4 2.7 %copy-start.1 = (f32[1,6,32]{2,0,1:T(1,128)S(1)}, f32[1,6,32]{2,0,1:T(1,128)}, u32[]{:S(2)}) copy-start(f32[1,6,32]{2,0,1:T(1,128)} %param.12) | copy-start | bytes 2308
  144.1 105.6 %all-gather.7.cloned.1.call-start = ((), (), s32[]{:S(2)}) async-start(), calls=%async_computation.2 | async-start | bytes 8192000 | tf_op jit(solution)/shard_map/all_gather | solution.py:55
  201.7 4.4 %copy-start = (f32[8,160,640]{2,0,1:T(8,128)S(1)}, f32[8,160,640]{2,0,1:T(8,128)}, u32[]{:S(2)}) copy-start(f32[8,160,640]{2,0,1:T(8,128)} %get-tuple-element.20) | copy-start | bytes 9830404
Sparse Core Ops, SparseCore 0:
  144.2 40.6 all-gather.4
  201.8 47.7 all-gather.6

commit v2 on v1

v2 whole, which is shorter than its diff:
```python
import functools
import jax
import jax.numpy as jnp
from jax import lax
from jax.experimental import pallas as pl
from jax.experimental.pallas import tpu as pltpu
from jax.sharding import PartitionSpec as P

MESH = pl.DeviceIdType.MESH
LANES = 128


def step_kernel(
    n_run, n_rep, nsys, held, chunks, chunk_rows, dout,
    slots, meta, coef_out, merge_coef, weights, moment1, moment2,
    weights_out, moment1_out, moment2_out, merged_out,
    land, meta_land, coef_land, sums, rounded, wbuf, fbuf, sbuf, mbuf,
    a2a_send, a2a_recv, meta_send, meta_recv, coef_send, coef_recv,
    x_send, x_recv, pair_send, pair_recv, own_sem, in_sem, out_sem,
):
    me = lax.axis_index("run")
    rep = lax.axis_index("rep")
    partner = rep + 1 - 2 * lax.rem(rep, 2)
    n_x = n_rep // 2
    experts = n_rep * held

    loads = [
        pltpu.make_async_copy(src, dst, in_sem.at[i])
        for i, (src, dst) in enumerate(((weights, wbuf), (moment1, fbuf), (moment2, sbuf)))
    ]
    for load in loads:
        load.start()
    own = pltpu.make_async_copy(slots.at[me], land.at[me], own_sem)
    own.start()

    barrier = pltpu.get_barrier_semaphore()
    for o in range(1, n_run):
        pl.semaphore_signal(
            barrier, inc=1, device_id={"run": lax.rem(me + o, n_run)}, device_id_type=MESH
        )
    for o in range(1, n_rep):
        pl.semaphore_signal(
            barrier, inc=1, device_id={"rep": lax.rem(rep + o, n_rep)}, device_id_type=MESH
        )
    pl.semaphore_wait(barrier, n_run + n_rep - 2)

    started = []

    def send(src, dst, send_sem, recv_sem, device):
        copy = pltpu.make_async_remote_copy(
            src_ref=src, dst_ref=dst, send_sem=send_sem, recv_sem=recv_sem,
            device_id=device, device_id_type=MESH,
        )
        copy.start()
        started.append(copy)
        return copy

    metas = [
        send(meta, meta_land.at[me], meta_send.at[o - 1], meta_recv.at[o - 1],
             {"run": lax.rem(me + o, n_run)})
        for o in range(1, n_run)
    ]
    coefs = []
    for o in range(1, n_rep):
        dest = lax.rem(rep + o, n_rep)
        coefs.append(
            send(coef_out.at[dest], coef_land.at[rep], coef_send.at[o - 1], coef_recv.at[o - 1],
                 {"rep": dest})
        )
    pieces = []
    for c in range(chunks):
        pieces.append([])
        for o in range(1, n_run):
            dest = lax.rem(me + o, n_run)
            pieces[c].append(
                send(slots.at[dest, c], land.at[me, c], a2a_send.at[c, o - 1],
                     a2a_recv.at[c, o - 1], {"run": dest})
            )

    meta_land[me] = meta[...]
    coef_land[rep] = coef_out[rep]
    own.wait()
    for copy in metas:
        copy.wait_recv()
    for copy in coefs:
        copy.wait_recv()
    for load in loads:
        load.wait()

    group = 16 if chunk_rows % 16 == 0 else chunk_rows
    lane_steps = dout // LANES

    def tiles(body):
        def step(i, carry):
            row = lax.div(i, lane_steps) * group
            lane = lax.rem(i, lane_steps) * LANES
            body(pl.multiple_of(row, group), pl.multiple_of(lane, LANES))
            return carry

        lax.fori_loop(0, (chunk_rows // group) * lane_steps, step, 0)

    def spread(buf, kind, c):
        direct = send(buf.at[c, rep], buf.at[c, rep], pair_send.at[kind, c, 0],
                      pair_recv.at[kind, c, 0], {"rep": partner})
        across = [
            send(buf.at[c, rep], buf.at[c, rep], x_send.at[kind, c, j - 1],
                 x_recv.at[kind, c, j - 1], {"rep": lax.rem(rep + 2 * j, n_rep)})
            for j in range(1, n_x)
        ]
        return direct, across

    def collect(buf, kind, c, direct, across):
        relays = []
        for j in range(1, n_x):
            across[j - 1].wait_recv()
            slot = lax.rem(rep + n_rep - 2 * j, n_rep)
            relays.append(
                send(buf.at[c, slot], buf.at[c, slot], pair_send.at[kind, c, j],
                     pair_recv.at[kind, c, j], {"rep": partner})
            )
        direct.wait_recv()
        for relay in relays:
            relay.wait_recv()

    def sum_systems(c):
        def body(row, lane):
            rows = pl.ds(row, group)
            total = [jnp.zeros((group, LANES), jnp.float32)] * nsys
            for k in range(n_run):
                low = land[k, c, rows, pl.ds(lane, LANES)].astype(jnp.float32)
                high = land[k, c, rows, pl.ds(lane + dout, LANES)].astype(jnp.float32)
                for s in range(nsys):
                    total[s] = (
                        total[s]
                        + meta_land[k, s + 1 : s + 2, :] * low
                        + meta_land[k, s : s + 1, :] * high
                    )
            for s in range(nsys):
                sums[c, rep, s, rows, pl.ds(lane, LANES)] = total[s].astype(jnp.bfloat16)

        tiles(body)

    def update(c):
        def body(row, lane):
            rows, lanes = pl.ds(row, group), pl.ds(lane, LANES)
            place = pl.ds(c * chunk_rows + row, group)
            grad = [jnp.zeros((group, LANES), jnp.float32)] * held
            for r in range(n_rep):
                for s in range(nsys):
                    part = sums[c, r, s, rows, lanes].astype(jnp.float32)
                    for e in range(held):
                        at = s * held + e
                        grad[e] = grad[e] + coef_land[r, at : at + 1, :] * part
            for e in range(held):
                new_first = 0.9 * fbuf[e, place, lanes] + 0.1 * grad[e]
                new_second = 0.999 * sbuf[e, place, lanes] + 0.001 * grad[e] * grad[e]
                corr_first = 1.0 - 0.9**10
                corr_second = 1.0 - 0.999**10
                new_weights = wbuf[e, place, lanes] - 0.01 * (new_first / corr_first) / (
                    jnp.sqrt(new_second / corr_second) + 1e-08
                )
                fbuf[e, place, lanes] = new_first
                sbuf[e, place, lanes] = new_second
                wbuf[e, place, lanes] = new_weights
                rounded[c, rep, e, rows, lanes] = new_weights.astype(jnp.bfloat16)

        tiles(body)

    def merge(c):
        def body(row, lane):
            rows, lanes = pl.ds(row, group), pl.ds(lane, LANES)
            total = [jnp.zeros((group, LANES), jnp.float32)] * nsys
            for r in range(n_rep):
                for e in range(held):
                    part = rounded[c, r, e, rows, lanes].astype(jnp.float32)
                    for s in range(nsys):
                        at = s * experts + r * held + e
                        total[s] = total[s] + merge_coef[at : at + 1, :] * part
            for s in range(nsys):
                mbuf[c, s, rows, lanes] = total[s].astype(jnp.bfloat16)

        tiles(body)

    stores = []

    def store(src, dst, kind, c):
        copy = pltpu.make_async_copy(src, dst, out_sem.at[kind, c])
        copy.start()
        stores.append(copy)

    def finish(c, moving):
        collect(rounded, 1, c, *moving)
        merge(c)
        store(mbuf.at[c], merged_out.at[:, pl.ds(c * chunk_rows, chunk_rows), :], 3, c)

    waiting = None
    for c in range(chunks):
        for copy in pieces[c]:
            copy.wait_recv()
        sum_systems(c)
        moving = spread(sums, 0, c)
        if waiting is not None:
            finish(c - 1, waiting)
        collect(sums, 0, c, *moving)
        update(c)
        waiting = spread(rounded, 1, c)
        place = pl.ds(c * chunk_rows, chunk_rows)
        store(wbuf.at[:, place, :], weights_out.at[:, place, :], 0, c)
        store(fbuf.at[:, place, :], moment1_out.at[:, place, :], 1, c)
        store(sbuf.at[:, place, :], moment2_out.at[:, place, :], 2, c)
    finish(chunks - 1, waiting)
    for copy in started:
        copy.wait_send()
    for copy in stores:
        copy.wait()


def on_device(
    n_run, n_rep,
    edge_feats, edge_grads, edge_system, edge_count, coef, weights, first_moment, second_moment
):
    feats = edge_feats[0]
    grads = edge_grads[0]
    system = edge_system[0]
    live_count = edge_count[0, 0]
    group_coef = coef[0]
    nsys, experts = group_coef.shape
    held, din_local, dout = weights.shape
    live = jnp.arange(system.shape[0]) < live_count
    first = system[0]
    empty = jnp.zeros_like(grads)
    lower = jnp.where((live & (system == first))[:, None], grads, empty)
    upper = jnp.where((live & (system == first + 1))[:, None], grads, empty)
    right = jnp.concatenate([lower, upper], axis=1)
    slots = lax.dot_general(
        feats, right, (((0,), (0,)), ((), ())), preferred_element_type=jnp.float32
    ).astype(jnp.bfloat16)

    chunk_rows = 32 if din_local % 32 == 0 else din_local
    chunks = din_local // chunk_rows
    slots = slots.reshape(n_run, chunks, chunk_rows, 2 * dout)
    meta_rows = -(-(nsys + 1) // 8) * 8
    marks = (jnp.arange(meta_rows) == first + 1).astype(jnp.float32)
    meta = jnp.broadcast_to(marks[:, None], (meta_rows, LANES))
    by_owner = group_coef.reshape(nsys, n_rep, held).transpose(1, 0, 2).reshape(n_rep, nsys * held)
    coef_out = jnp.broadcast_to(by_owner[:, :, None], (n_rep, nsys * held, LANES))
    merge_coef = jnp.broadcast_to(
        group_coef.reshape(nsys * experts)[:, None], (nsys * experts, LANES)
    )

    bf16, f32 = jnp.bfloat16, jnp.float32
    dma = pltpu.SemaphoreType.DMA
    n_x = n_rep // 2
    anywhere = pl.BlockSpec(memory_space=pl.ANY)
    vmem = pl.BlockSpec(memory_space=pltpu.VMEM)
    block = jax.ShapeDtypeStruct(weights.shape, f32)
    outs = pl.pallas_call(
        functools.partial(step_kernel, n_run, n_rep, nsys, held, chunks, chunk_rows, dout),
        out_shape=(block, block, block, jax.ShapeDtypeStruct((nsys, din_local, dout), bf16)),
        in_specs=[anywhere, vmem, vmem, vmem, anywhere, anywhere, anywhere],
        out_specs=(anywhere,) * 4,
        scratch_shapes=[
            pltpu.VMEM(slots.shape, bf16),
            pltpu.VMEM((n_run, meta_rows, LANES), f32),
            pltpu.VMEM(coef_out.shape, f32),
            pltpu.VMEM((chunks, n_rep, nsys, chunk_rows, dout), bf16),
            pltpu.VMEM((chunks, n_rep, held, chunk_rows, dout), bf16),
            pltpu.VMEM(weights.shape, f32),
            pltpu.VMEM(weights.shape, f32),
            pltpu.VMEM(weights.shape, f32),
            pltpu.VMEM((chunks, nsys, chunk_rows, dout), bf16),
            dma((chunks, n_run - 1)),
            dma((chunks, n_run - 1)),
            dma((n_run - 1,)),
            dma((n_run - 1,)),
            dma((n_rep - 1,)),
            dma((n_rep - 1,)),
            dma((2, chunks, n_x)),
            dma((2, chunks, n_x)),
            dma((2, chunks, n_x)),
            dma((2, chunks, n_x)),
            dma,
            dma((3,)),
            dma((4, chunks)),
        ],
        compiler_params=pltpu.CompilerParams(
            collective_id=0, has_side_effects=True, vmem_limit_bytes=56 * 1024 * 1024
        ),
        name="exchange_step",
    )(slots, meta, coef_out, merge_coef, weights, first_moment, second_moment)
    return (*outs[:3], outs[3][None])


def solution(mesh):
    placed = (
        P("rep", "run", None),
        P("rep", "run", None),
        P("rep", "run"),
        P("rep", "run"),
        P("rep", None, None),
        P("rep", "run", None),
        P("rep", "run", None),
        P("rep", "run", None),
    )
    return jax.shard_map(
        functools.partial(on_device, mesh.shape["run"], mesh.shape["rep"]),
        mesh=mesh,
        in_specs=placed,
        out_specs=(
            P("rep", "run", None),
            P("rep", "run", None),
            P("rep", "run", None),
            P("rep", None, "run", None),
        ),
        check_vma=False,
    )
```

time: 266 us -> 160 us (0.60)
  Pallas kernels: 0 us -> 129 us
  blocking collectives: 74.9 us -> 0 us
  waiting for transfers between devices: 73.9 us -> 0 us
  between operations: 50.7 us -> 1.99 us
  matrix products: 28 us -> 8.53 us
  other arithmetic: 13 us -> 5.83 us
  starting transfers between devices: 5.84 us -> 0 us
  local copies, waits for them, and re-layouts: 17.5 us -> 13.9 us
    pallas_call x0 -> x1, Pallas kernels: none -> 129 us  [on_device(): pl.pallas_call(functools.partial(step_kernel, n_run, n_rep, nsys, held, c...]
    all_gather x2 -> x0, waiting for transfers between devices: 73.8 us -> none  [the longest x1 38.9 us: on_device(): every_expert = lax.all_gather(rounded, 'rep', axis=0, tiled=True)]
    unnamed x1 -> x0, blocking collectives: 69.2 us -> none
    dot_general x2 -> x0, matrix products: 19.5 us -> none  [the longest x1 16.8 us: on_device(): jnp.einsum('ge,gio->eio', own_coef, every_sum.astype(jnp.float32), precis...]
    unnamed x5 -> x1, other arithmetic: 6.61 us -> 0.7 us
    all_to_all x1 -> x0, starting transfers between devices: 5.79 us -> none  [on_device(): lax.all_to_all(slots, 'run', split_axis=0, concat_axis=0, tiled=True)]
    all_gather x1 -> x0, blocking collectives: 5.74 us -> none  [on_device(): every_coef = lax.all_gather(group_coef, 'rep', axis=0, tiled=True)]
    reshape x1 -> x0, local copies, waits for them, and re-layouts: 3.42 us -> none  [on_device(): flat = every_expert.astype(jnp.float32).reshape(experts, din_local * dout)]
  transfers between devices with their start and end apart: 3 -> 0, of which waited for: 2 -> 0; matrix products, arithmetic and copies ran while one was open for 4% -> 0% of each run, Pallas kernels for 0% -> 0%
where the time goes in v2:
time: 160 us
  Pallas kernels  129 us (81%)
  local copies, waits for them, and re-layouts  13.9 us (9%)
  matrix products  8.53 us (5%)
  other arithmetic  5.83 us (4%)
  between operations  1.99 us (1%)
    pallas_call x1, Pallas kernels, on_device(): pl.pallas_call(functools.partial(step_kernel, n_run, n_rep, nsys, held, c...  129 us
    unnamed x12, local copies, waits for them, and re-layouts  10.3 us
    dot_general x1, matrix products, on_device(): lax.dot_general(feats, right, (((0,), (0,)), ((), ())), preferred_element...  8.53 us
    select_n x1, other arithmetic, on_device(): lower = jnp.where((live & (system == first))[:, None], grads, empty)  3.72 us

profile of v2, /device:TPU:13, one launch (start us, length us, event | category | flops | bytes accessed | tf_op | source)
XLA Modules:
  0.0 159.6 jit_solution(4849730194491537703)
XLA Ops:
  1.3 1.2 slice.4
  3.1 1.4 compare_reduce_fusion.1
  4.5 0.7 broadcast_in_dim.44.meta
  5.2 0.7 reduce.2
  5.9 0.1 broadcast_in_dim.47
  6.0 0.1 reshape_squeeze.3
  6.0 0.1 broadcast_in_dim.45
  6.1 0.7 broadcast_in_dim.46.coef_out
  6.9 0.7 broadcast_in_dim.48.merge_coef
  7.6 0.0 copy-start.3
  7.6 3.7 %bitcast_select_fusion.1 = (bf16[2048,640]{1,0:T(8,128)(2,1)S(1)}, bf16[2048,640]{1,0:T(8,128)(2,1)S(1)}) fusion(bf16[1,2048,640]{2,1,0:T(8,128)(2,1)} %param.9, pred[2048]{0:T(1024)(128)(4,1)S(1)} %get-tuple-element.17, pred[2048]{0:T(1024)(128)(4,1)S(1)} %get-tuple-element.16), kind=kLoop, calls=%fused_computation.6 | loop fusion | flops 2621440 | bytes 7868416 | tf_op jit(solution)/shard_map/jit(_where)/select_n | solution.py:232
  11.3 0.0 copy-done.3
  11.3 8.5 %convolution_convert_fusion = bf16[1280,1280]{0,1:T(8,128)(2,1)} fusion(bf16[2048,640]{1,0:T(8,128)(2,1)S(1)} %get-tuple-element.15, bf16[2048,640]{1,0:T(8,128)(2,1)S(1)} %get-tuple-element.14, bf16[1,2048,1280]{2,1,0:T(8,128)(2,1)S(1)} %copy-done.3), kind=kOutput, calls=%fused_computation | convolution fusion | flops 6723010560 | bytes 13762560 | tf_op jit(solution)/shard_map/dot_general | solution.py:235
  19.9 129.3 %exchange_step.1 = (f32[8,160,640]{2,1,0:T(8,128)}, f32[8,160,640]{2,1,0:T(8,128)}, f32[8,160,640]{2,1,0:T(8,128)}, bf16[6,160,640]{2,1,0:T(8,128)(2,1)}) custom-call(bf16[8,5,32,1280]{3,2,1,0:T(8,128)(2,1)} %bitcast.16, f32[8,128]{1,0:T(8,128)} %broadcast_in_dim.44.meta, f32[4,48,128]{2,1,0:T(8,128)} %broadcast_in_dim.46.coef_out, ...), custom_call_target="tpu_custom_call" | custom-call | tf_op jit(solution)/shard_map/exchange_step/pallas_call | solution.py:257
  149.2 0.0 copy-start.1
  149.2 4.0 %copy.21 = f32[8,160,640]{2,1,0:T(8,128)} copy(f32[8,160,640]{2,1,0:T(8,128)} %get-tuple-element.22) | data formatting | bytes 6553600
  153.3 0.0 copy-done.1
  153.3 0.0 copy-start
  153.3 1.7 %copy.22 = f32[8,160,640]{2,1,0:T(8,128)} copy(f32[8,160,640]{2,1,0:T(8,128)S(1)} %copy-done.1) | data formatting | bytes 6553600
  155.0 1.4 copy-done
  156.4 0.0 copy-start.2
  156.4 1.7 %copy.23 = f32[8,160,640]{2,1,0:T(8,128)} copy(f32[8,160,640]{2,1,0:T(8,128)S(1)} %copy-done) | data formatting | bytes 6553600
  158.1 0.5 copy-done.2
  158.5 1.0 copy.24
  (3 shorter events, 0.0 us)
Async XLA Ops:
  7.6 3.7 %copy-start.3 = (bf16[1,2048,1280]{2,1,0:T(8,128)(2,1)S(1)}, bf16[1,2048,1280]{2,1,0:T(8,128)(2,1)}, u32[]{:S(2)}) copy-start(bf16[1,2048,1280]{2,1,0:T(8,128)(2,1)} %param.8) | copy-start | bytes 15728644
  149.2 4.0 %copy-start.1 = (f32[8,160,640]{2,1,0:T(8,128)S(1)}, f32[8,160,640]{2,1,0:T(8,128)}, u32[]{:S(2)}) copy-start(f32[8,160,640]{2,1,0:T(8,128)} %get-tuple-element.23) | copy-start | bytes 9830404
  153.3 3.1 %copy-start = (f32[8,160,640]{2,1,0:T(8,128)S(1)}, f32[8,160,640]{2,1,0:T(8,128)}, u32[]{:S(2)}) copy-start(f32[8,160,640]{2,1,0:T(8,128)} %get-tuple-element.24) | copy-start | bytes 9830404
  156.4 2.2 %copy-start.2 = (bf16[6,160,640]{2,1,0:T(8,128)(2,1)S(1)}, bf16[6,160,640]{2,1,0:T(8,128)(2,1)}, u32[]{:S(2)}) copy-start(bf16[6,160,640]{2,1,0:T(8,128)(2,1)} %get-tuple-element.11) | copy-start | bytes 3686404

commit v3 on v2

--- a/solution.py
+++ b/solution.py
@@ -68,14 +68,21 @@
                  {"rep": dest})
         )
     pieces = []
-    for c in range(chunks):
+
+    def scatter(c):
+        if c >= chunks:
+            return
         pieces.append([])
         for o in range(1, n_run):
-            dest = lax.rem(me + o, n_run)
+            dest = jnp.bitwise_xor(me, o)
             pieces[c].append(
                 send(slots.at[dest, c], land.at[me, c], a2a_send.at[c, o - 1],
                      a2a_recv.at[c, o - 1], {"run": dest})
             )
+
+    ahead = 1
+    for c in range(ahead):
+        scatter(c)
 
     meta_land[me] = meta[...]
     coef_land[rep] = coef_out[rep]
@@ -199,6 +206,7 @@
             copy.wait_recv()
         sum_systems(c)
         moving = spread(sums, 0, c)
+        scatter(c + ahead)
         if waiting is not None:
             finish(c - 1, waiting)
         collect(sums, 0, c, *moving)

time: 160 us -> 145 us (0.906)
  Pallas kernels: 129 us -> 113 us
    pallas_call x1, Pallas kernels: 129 us -> 113 us  [on_device(): pl.pallas_call(functools.partial(step_kernel, n_run, n_rep, nsys, held, c...]
where the time goes in v3:
time: 145 us; the launch traced here: 143 us
  Pallas kernels  113 us (78%)
  local copies, waits for them, and re-layouts  13.9 us (10%)
  matrix products  8.53 us (6%)
  other arithmetic  5.83 us (4%)
  between operations  1.99 us (1%)
    pallas_call x1, Pallas kernels, on_device(): pl.pallas_call(functools.partial(step_kernel, n_run, n_rep, nsys, held, c...  113 us
    unnamed x12, local copies, waits for them, and re-layouts  10.3 us
    dot_general x1, matrix products, on_device(): lax.dot_general(feats, right, (((0,), (0,)), ((), ())), preferred_element...  8.53 us
    select_n x1, other arithmetic, on_device(): lower = jnp.where((live & (system == first))[:, None], grads, empty)  3.72 us

profile of v3, /device:TPU:13, one launch (start us, length us, event | category | flops | bytes accessed | tf_op | source)
XLA Modules:
  0.0 143.2 jit_solution(9052423319386039900)
XLA Ops:
  1.3 1.2 slice.4
  3.1 1.4 compare_reduce_fusion.1
  4.5 0.7 broadcast_in_dim.44.meta
  5.2 0.7 reduce.2
  5.9 0.1 broadcast_in_dim.47
  6.0 0.1 reshape_squeeze.3
  6.0 0.1 broadcast_in_dim.45
  6.1 0.7 broadcast_in_dim.46.coef_out
  6.9 0.7 broadcast_in_dim.48.merge_coef
  7.6 0.0 copy-start.3
  7.6 3.7 %bitcast_select_fusion.1 = (bf16[2048,640]{1,0:T(8,128)(2,1)S(1)}, bf16[2048,640]{1,0:T(8,128)(2,1)S(1)}) fusion(bf16[1,2048,640]{2,1,0:T(8,128)(2,1)} %param.9, pred[2048]{0:T(1024)(128)(4,1)S(1)} %get-tuple-element.17, pred[2048]{0:T(1024)(128)(4,1)S(1)} %get-tuple-element.16), kind=kLoop, calls=%fused_computation.6 | loop fusion | flops 2621440 | bytes 7868416 | tf_op jit(solution)/shard_map/jit(_where)/select_n | solution.py:240
  11.3 0.0 copy-done.3
  11.3 8.5 %convolution_convert_fusion = bf16[1280,1280]{0,1:T(8,128)(2,1)} fusion(bf16[2048,640]{1,0:T(8,128)(2,1)S(1)} %get-tuple-element.15, bf16[2048,640]{1,0:T(8,128)(2,1)S(1)} %get-tuple-element.14, bf16[1,2048,1280]{2,1,0:T(8,128)(2,1)S(1)} %copy-done.3), kind=kOutput, calls=%fused_computation | convolution fusion | flops 6723010560 | bytes 13762560 | tf_op jit(solution)/shard_map/dot_general | solution.py:243
  19.9 113.0 %exchange_step.1 = (f32[8,160,640]{2,1,0:T(8,128)}, f32[8,160,640]{2,1,0:T(8,128)}, f32[8,160,640]{2,1,0:T(8,128)}, bf16[6,160,640]{2,1,0:T(8,128)(2,1)}) custom-call(bf16[8,5,32,1280]{3,2,1,0:T(8,128)(2,1)} %bitcast.16, f32[8,128]{1,0:T(8,128)} %broadcast_in_dim.44.meta, f32[4,48,128]{2,1,0:T(8,128)} %broadcast_in_dim.46.coef_out, ...), custom_call_target="tpu_custom_call" | custom-call | tf_op jit(solution)/shard_map/exchange_step/pallas_call | solution.py:265
  132.8 0.0 copy-start.1
  132.9 4.0 %copy.21 = f32[8,160,640]{2,1,0:T(8,128)} copy(f32[8,160,640]{2,1,0:T(8,128)} %get-tuple-element.22) | data formatting | bytes 6553600
  136.9 0.0 copy-done.1
  136.9 0.0 copy-start
  136.9 1.7 %copy.22 = f32[8,160,640]{2,1,0:T(8,128)} copy(f32[8,160,640]{2,1,0:T(8,128)S(1)} %copy-done.1) | data formatting | bytes 6553600
  138.6 1.4 copy-done
  140.0 0.0 copy-start.2
  140.0 1.7 %copy.23 = f32[8,160,640]{2,1,0:T(8,128)} copy(f32[8,160,640]{2,1,0:T(8,128)S(1)} %copy-done) | data formatting | bytes 6553600
  141.7 0.5 copy-done.2
  142.2 1.0 copy.24
  (3 shorter events, 0.0 us)
Async XLA Ops:
  7.6 3.7 %copy-start.3 = (bf16[1,2048,1280]{2,1,0:T(8,128)(2,1)S(1)}, bf16[1,2048,1280]{2,1,0:T(8,128)(2,1)}, u32[]{:S(2)}) copy-start(bf16[1,2048,1280]{2,1,0:T(8,128)(2,1)} %param.8) | copy-start | bytes 15728644
  132.8 4.0 %copy-start.1 = (f32[8,160,640]{2,1,0:T(8,128)S(1)}, f32[8,160,640]{2,1,0:T(8,128)}, u32[]{:S(2)}) copy-start(f32[8,160,640]{2,1,0:T(8,128)} %get-tuple-element.23) | copy-start | bytes 9830404
  136.9 3.1 %copy-start = (f32[8,160,640]{2,1,0:T(8,128)S(1)}, f32[8,160,640]{2,1,0:T(8,128)}, u32[]{:S(2)}) copy-start(f32[8,160,640]{2,1,0:T(8,128)} %get-tuple-element.24) | copy-start | bytes 9830404
  140.0 2.2 %copy-start.2 = (bf16[6,160,640]{2,1,0:T(8,128)(2,1)S(1)}, bf16[6,160,640]{2,1,0:T(8,128)(2,1)}, u32[]{:S(2)}) copy-start(bf16[6,160,640]{2,1,0:T(8,128)(2,1)} %get-tuple-element.11) | copy-start | bytes 3686404
